TPU v7x, 256 devices: a whole 4x4x8 slice. The times are simulated.
256 devices in a mesh: grid: 16 (over z, y_lo), chan: 16 (over x, y_hi, core).
Axes of the slice: x: 4, y: 4 (y_hi: 2, y_lo: 2; y = y_hi * 2 + y_lo), z: 8, core: 2. Of those that a mesh axis runs over, the one named last changes fastest.
Arguments:
- spectra: bfloat16 [2, 8, 48, 4096], P(None, None, 'grid', 'chan'), may hold values from -90 to 90, as said below
- travel: int32 [65536, 4096], P('grid', 'chan'), may hold values from 0 to 2047
- quality: int32 [4096], P('chan'), may hold values 0 or 1
Outputs:
- beam_power: float32 [48, 65536], P(None, ('grid', 'chan'))
Inputs may be any that keep to these rules, and one draw needn't show every extreme that they name: `spectra`: spectra of the windows; scales differ between channels and between windows.
All inputs are finite; a program needn't handle non-finite values. No bound on the sum of `quality` on one device may be relied on, other than what follows from the above.
Results may differ from a plain program's by a relative error of at most 0.0012.
Values may be sent and summed in bfloat16 or wider, within the bound.
No kernel may reach another device: no remote copies, remote signals or barrier semaphores. Data moves between devices by JAX's collectives and lax.ppermute only.
A program may use at most 64 MiB of HBM per device.

v0:
```python
import math
import jax
import jax.numpy as jnp
from jax import lax
from jax.sharding import PartitionSpec as P

NFFT = 2048
lowest_bin = 37
bin_spacing = 29


def replica_rows(delay_rows, freq_count):
    freq_bins = lowest_bin + bin_spacing * jnp.arange(freq_count, dtype=jnp.int32)
    phase_index = freq_bins[:, None, None] * delay_rows[None, :, :] % NFFT
    angles = phase_index.astype(jnp.float32) * (2.0 * math.pi / NFFT)
    return jnp.concatenate([jnp.cos(angles), jnp.sin(angles)], axis=2).astype(jnp.bfloat16)


def stacked_spectra(masked):
    real_part = masked[0]
    imag_part = masked[1]
    upper_half = jnp.concatenate([real_part, imag_part], axis=1)
    lower_half = jnp.concatenate([-imag_part, real_part], axis=1)
    return jnp.concatenate([upper_half, lower_half], axis=2)


def beams_for(delay_table, spectra_matrix, freq_count):
    total_rows = delay_table.shape[0]
    chan_width = delay_table.shape[1]
    block_rows = math.gcd(total_rows, 1024)

    def one_block(delay_rows):
        replicas = replica_rows(delay_rows, freq_count)
        beam_terms = jnp.einsum(
            "frk,fwk->rfw", replicas, spectra_matrix, preferred_element_type=jnp.float32
        )
        return beam_terms.reshape(block_rows, -1)

    block_terms = lax.map(
        one_block, delay_table.reshape(total_rows // block_rows, block_rows, chan_width)
    )
    return block_terms.reshape(total_rows, -1)


def per_device(spectra, travel, quality):
    freq_count = spectra.shape[1]
    masked = spectra * quality.astype(jnp.bfloat16)
    channel_count = masked.shape[3] * lax.axis_size("chan")
    gathered = lax.all_gather(masked, "grid", axis=2, tiled=True)
    window_count = gathered.shape[2]
    norm_sum = lax.psum(jnp.sum(gathered.astype(jnp.float32) ** 2, axis=(0, 1, 3)), "chan")
    window_norm = norm_sum / (freq_count * channel_count) + 1e-06
    rows_out = travel.shape[0] // lax.axis_size("chan")
    spectra_matrix = stacked_spectra(gathered)
    beam_sums = lax.psum_scatter(
        beams_for(travel, spectra_matrix, freq_count), "chan", scatter_dimension=0, tiled=True
    )
    energies = jnp.sum(beam_sums.reshape(rows_out, 2 * freq_count, window_count) ** 2, axis=1)
    beam_power = energies / (freq_count * channel_count * window_norm[None, :])
    return beam_power.T


def solution(mesh):
    return jax.shard_map(
        per_device,
        mesh=mesh,
        in_specs=(P(None, None, "grid", "chan"), P("grid", "chan"), P("chan")),
        out_specs=P(None, ("grid", "chan")),
        check_vma=False,
    )
```

profile of v0, /device:TPU:1, one launch (start us, length us, event | category | flops | bytes accessed | tf_op | source)
XLA Modules:
  0.0 362.6 jit_solution(12810021472243952818)
XLA Ops:
  6.5 0.7 convert_element_type.16
  7.2 0.7 copy_multiply_fusion
  8.0 32.6 %all_gather.3 = bf16[2,8,48,256]{3,1,0,2:T(8,128)(2,1)S(1)} all-gather(bf16[2,8,3,256]{3,1,0,2:T(8,128)(2,1)S(1)} %copy_multiply_fusion), channel_id=1, replica_groups=mesh['grid'=16,'chan'=16] {'grid'}, dimensions={2}, use_global_device_ids=true | all-gather | bytes 417792 | tf_op jit(solution)/shard_map/all_gather | solution.py:49
  40.6 0.1 maximum_maximum_fusion
  40.7 1.1 copy.10
  41.8 177.9 %while.12 = (s32[]{:T(128)}, f32[4,1024,768]{2,1,0:T(8,128)}, s32[4,1024,256]{2,1,0:T(8,128)}, bf16[8,96,512]{2,1,0:T(8,128)(2,1)}, s32[]{:T(128)}) while((s32[]{:T(128)}, f32[4,1024,768]{2,1,0:T(8,128)}, s32[4,1024,256]{2,1,0:T(8,128)}, bf16[8,96,512]{2,1,0:T(8,128)(2,1)}, s32[]{:T(128)}) %tuple.36), condition=%wide.region_1.0_spmd, body=%wide.region_0.0_spmd.sunk | while | flops 855638016 | bytes 36438156 | solution.py:39
  41.8 1.3 dynamic-slice_bitcast_fusion.2
  43.1 33.8 %cosine_convert_fusion.2 = (bf16[8,1024,256]{2,1,0:T(8,128)(2,1)S(1)}, bf16[8,1024,256]{2,1,0:T(8,128)(2,1)S(1)}) fusion(s32[1024,256]{1,0:T(8,128)S(1)} %dynamic-slice_bitcast_fusion.2, s32[8]{0:T(128)S(1)} %multiply_add_fusion.2), kind=kLoop, calls=%fused_computation.13.clone.1 | loop fusion | flops 33554432 | bytes 9437216 | tf_op jit(solution)/shard_map/convert
  76.9 5.1 %fusion.15 = f32[8,1024,96]{1,2,0:T(8,128)} fusion(bf16[8,96,512]{2,1,0:T(8,128)(2,1)} %get-tuple-element.118, bf16[8,1024,256]{2,1,0:T(8,128)(2,1)S(1)} %get-tuple-element.103, bf16[8,1024,256]{2,1,0:T(8,128)(2,1)S(1)} %get-tuple-element.104), kind=kOutput, calls=%fused_computation.8.clone.1 | convolution fusion | flops 822083584 | bytes 12320768 | tf_op jit(solution)/shard_map/while/body/eval_jaxpr/frk,fwk->rfw/dot_general | solution.py:34
  82.0 2.4 copy.20
  84.4 1.9 constant_dynamic-update-slice_fusion.2
  86.3 1.3 dynamic-slice_bitcast_fusion.2
  87.6 33.8 %cosine_convert_fusion.2 = (bf16[8,1024,256]{2,1,0:T(8,128)(2,1)S(1)}, bf16[8,1024,256]{2,1,0:T(8,128)(2,1)S(1)}) fusion(s32[1024,256]{1,0:T(8,128)S(1)} %dynamic-slice_bitcast_fusion.2, s32[8]{0:T(128)S(1)} %multiply_add_fusion.2), kind=kLoop, calls=%fused_computation.13.clone.1 | loop fusion | flops 33554432 | bytes 9437216 | tf_op jit(solution)/shard_map/convert
  121.4 5.1 %fusion.15 = f32[8,1024,96]{1,2,0:T(8,128)} fusion(bf16[8,96,512]{2,1,0:T(8,128)(2,1)} %get-tuple-element.118, bf16[8,1024,256]{2,1,0:T(8,128)(2,1)S(1)} %get-tuple-element.103, bf16[8,1024,256]{2,1,0:T(8,128)(2,1)S(1)} %get-tuple-element.104), kind=kOutput, calls=%fused_computation.8.clone.1 | convolution fusion | flops 822083584 | bytes 12320768 | tf_op jit(solution)/shard_map/while/body/eval_jaxpr/frk,fwk->rfw/dot_general | solution.py:34
  126.5 2.4 copy.20
  128.9 1.9 constant_dynamic-update-slice_fusion.2
  130.8 1.3 dynamic-slice_bitcast_fusion.2
  132.1 33.8 %cosine_convert_fusion.2 = (bf16[8,1024,256]{2,1,0:T(8,128)(2,1)S(1)}, bf16[8,1024,256]{2,1,0:T(8,128)(2,1)S(1)}) fusion(s32[1024,256]{1,0:T(8,128)S(1)} %dynamic-slice_bitcast_fusion.2, s32[8]{0:T(128)S(1)} %multiply_add_fusion.2), kind=kLoop, calls=%fused_computation.13.clone.1 | loop fusion | flops 33554432 | bytes 9437216 | tf_op jit(solution)/shard_map/convert
  165.9 5.1 %fusion.15 = f32[8,1024,96]{1,2,0:T(8,128)} fusion(bf16[8,96,512]{2,1,0:T(8,128)(2,1)} %get-tuple-element.118, bf16[8,1024,256]{2,1,0:T(8,128)(2,1)S(1)} %get-tuple-element.103, bf16[8,1024,256]{2,1,0:T(8,128)(2,1)S(1)} %get-tuple-element.104), kind=kOutput, calls=%fused_computation.8.clone.1 | convolution fusion | flops 822083584 | bytes 12320768 | tf_op jit(solution)/shard_map/while/body/eval_jaxpr/frk,fwk->rfw/dot_general | solution.py:34
  171.0 2.4 copy.20
  173.4 1.9 constant_dynamic-update-slice_fusion.2
  175.3 1.3 dynamic-slice_bitcast_fusion.2
  176.6 33.8 %cosine_convert_fusion.2 = (bf16[8,1024,256]{2,1,0:T(8,128)(2,1)S(1)}, bf16[8,1024,256]{2,1,0:T(8,128)(2,1)S(1)}) fusion(s32[1024,256]{1,0:T(8,128)S(1)} %dynamic-slice_bitcast_fusion.2, s32[8]{0:T(128)S(1)} %multiply_add_fusion.2), kind=kLoop, calls=%fused_computation.13.clone.1 | loop fusion | flops 33554432 | bytes 9437216 | tf_op jit(solution)/shard_map/convert
  210.4 5.1 %fusion.15 = f32[8,1024,96]{1,2,0:T(8,128)} fusion(bf16[8,96,512]{2,1,0:T(8,128)(2,1)} %get-tuple-element.118, bf16[8,1024,256]{2,1,0:T(8,128)(2,1)S(1)} %get-tuple-element.103, bf16[8,1024,256]{2,1,0:T(8,128)(2,1)S(1)} %get-tuple-element.104), kind=kOutput, calls=%fused_computation.8.clone.1 | convolution fusion | flops 822083584 | bytes 12320768 | tf_op jit(solution)/shard_map/while/body/eval_jaxpr/frk,fwk->rfw/dot_general | solution.py:34
  215.5 2.4 copy.20
  217.9 1.8 constant_dynamic-update-slice_fusion.2
  219.7 0.4 multiply_reduce_fusion
  220.2 39.9 %psum.7 = f32[48]{0:T(128)S(1)} all-reduce(f32[48]{0:T(128)S(1)} %multiply_reduce_fusion), channel_id=1, replica_groups=mesh['grid'=16,'chan'=16] {'chan'}, use_global_device_ids=true, to_apply=%region_5.6 | all-reduce | flops 48 | bytes 384 | tf_op jit(solution)/shard_map/psum | solution.py:51
  260.1 93.1 %reduce-scatter.2.cloned.1.call-done = f32[256,768]{1,0:T(8,128)} async-done(((f32[4096,768]{1,0:T(8,128)}), f32[256,768]{1,0:T(8,128)}) %reduce-scatter.2.cloned.1.call-update) | async-done | bytes 786448 | tf_op jit(solution)/shard_map/reduce_scatter | solution.py:55
  353.3 1.5 integer_pow.9
  354.7 0.3 copy.12
  355.1 0.7 divide_bitcast_fusion
  (11 shorter events, 0.1 us)
Async XLA Ops:
  6.5 346.7 %reduce-scatter.2.cloned.1.call-start = ((), (), s32[]{:S(2)}) async-start(), calls=%async_computation.1 | async-start | bytes 13369344 | tf_op jit(solution)/shard_map/reduce_scatter | solution.py:55
Sparse Core Ops, SparseCore 0:
  219.9 133.3 reduce-scatter.1
where the time goes:
time: 363 us
  other arithmetic  139 us (38%)
  waiting for transfers between devices  93.2 us (26%)
  blocking collectives  72.5 us (20%)
  local copies, waits for them, and re-layouts  23.6 us (7%)
  matrix products  20.4 us (6%)
  between operations  13.4 us (4%)
    another operation x4, other arithmetic  135 us
    reduce_scatter x1, waiting for transfers between devices, per_device(): lax.psum_scatter(beams_for(travel, spectra_matrix, freq_count), 'chan', s...  93.1 us
    psum x1, blocking collectives, per_device(): lax.psum(jnp.sum(gathered.astype(jnp.float32) ** 2, axis=(0, 1, 3)), 'chan')  39.9 us
    all_gather x1, blocking collectives, per_device(): gathered = lax.all_gather(masked, 'grid', axis=2, tiled=True)  32.6 us
    dot_general x4, matrix products, one_block(): jnp.einsum('frk,fwk->rfw', replicas, spectra_matrix, preferred_element_ty...  20.4 us
    dynamic_update_slice x8, local copies, waits for them, and re-layouts, beams_for(): lax.map(one_block, delay_table.reshape(total_rows // block_rows, block_ro...  17 us
  transfers between devices with their start and end apart: 1, of which 1 were waited for; matrix products, arithmetic and copies ran while one was open for 0% of the time, Pallas kernels for 0%

commit v1 on v0

--- a/solution.py
+++ b/solution.py
@@ -46,7 +46,9 @@
     freq_count = spectra.shape[1]
     masked = spectra * quality.astype(jnp.bfloat16)
     channel_count = masked.shape[3] * lax.axis_size("chan")
-    gathered = lax.all_gather(masked, "grid", axis=2, tiled=True)
+    gathered = jnp.concatenate(
+        lax.all_to_all(jnp.stack([masked] * lax.axis_size("grid"), axis=0), "grid", 0, 0), axis=2
+    )
     window_count = gathered.shape[2]
     norm_sum = lax.psum(jnp.sum(gathered.astype(jnp.float32) ** 2, axis=(0, 1, 3)), "chan")
     window_norm = norm_sum / (freq_count * channel_count) + 1e-06

time: 363 us -> 349 us (0.961)
  blocking collectives: 72.5 us -> 34.7 us
  waiting for transfers between devices: 93.2 us -> 106 us
  starting transfers between devices: 0.01 us -> 10.2 us
    all_gather x1 -> x0, blocking collectives: 32.6 us -> none  [per_device(): gathered = lax.all_gather(masked, 'grid', axis=2, tiled=True)]
    all_to_all x0 -> x1, waiting for transfers between devices: none -> 13.2 us  [per_device(): lax.all_to_all(jnp.stack([masked] * lax.axis_size('grid'), axis=0), 'grid...]
    all_to_all x0 -> x1, starting transfers between devices: none -> 10.1 us  [per_device(): lax.all_to_all(jnp.stack([masked] * lax.axis_size('grid'), axis=0), 'grid...]
    psum x1, blocking collectives: 39.9 us -> 34.7 us  [per_device(): lax.psum(jnp.sum(gathered.astype(jnp.float32) ** 2, axis=(0, 1, 3)), 'chan')]
  transfers between devices with their start and end apart: 1 -> 2, of which waited for: 1 -> 2; matrix products, arithmetic and copies ran while one was open for 0% -> 0% of each run, Pallas kernels for 0% -> 0%
where the time goes in v1:
time: 349 us
  other arithmetic  139 us (40%)
  waiting for transfers between devices  106 us (30%)
  blocking collectives  34.7 us (10%)
  local copies, waits for them, and re-layouts  24.5 us (7%)
  matrix products  20.4 us (6%)
  between operations  13.5 us (4%)
  starting transfers between devices  10.2 us (3%)
    another operation x4, other arithmetic  135 us
    reduce_scatter x1, waiting for transfers between devices, per_device(): lax.psum_scatter(beams_for(travel, spectra_matrix, freq_count), 'chan', s...  92.9 us
    psum x1, blocking collectives, per_device(): lax.psum(jnp.sum(gathered.astype(jnp.float32) ** 2, axis=(0, 1, 3)), 'chan')  34.7 us
    dot_general x4, matrix products, one_block(): jnp.einsum('frk,fwk->rfw', replicas, spectra_matrix, preferred_element_ty...  20.4 us
    dynamic_update_slice x8, local copies, waits for them, and re-layouts, beams_for(): lax.map(one_block, delay_table.reshape(total_rows // block_rows, block_ro...  17 us
    all_to_all x1, waiting for transfers between devices, per_device(): lax.all_to_all(jnp.stack([masked] * lax.axis_size('grid'), axis=0), 'grid...  13.2 us
    all_to_all x1, starting transfers between devices, per_device(): lax.all_to_all(jnp.stack([masked] * lax.axis_size('grid'), axis=0), 'grid...  10.1 us
  transfers between devices with their start and end apart: 2, of which 2 were waited for; matrix products, arithmetic and copies ran while one was open for 0% of the time, Pallas kernels for 0%

profile of v1, /device:TPU:1, one launch (start us, length us, event | category | flops | bytes accessed | tf_op | source)
XLA Modules:
  0.0 348.6 jit_solution(12883207758132385941)
XLA Ops:
  6.5 0.7 convert_element_type.17
  7.2 0.7 broadcast_multiply_fusion
  8.0 0.8 stack.2
  8.8 10.1 %all-to-all-start = ((bf16[16,2,8,3,256]{4,2,3,1,0:T(8,128)(2,1)}), bf16[16,2,8,3,256]{4,2,3,1,0:T(8,128)(2,1)S(1)}, u32[]{:S(2)}, u32[]{:S(2)}) async-start(bf16[16,2,8,3,256]{4,2,3,1,0:T(8,128)(2,1)} %stack.2), calls=%async_computation | async-start | bytes 786432 | tf_op jit(solution)/shard_map/all_to_all | solution.py:50
  19.0 13.2 %all-to-all-done = bf16[16,2,8,3,256]{4,2,3,1,0:T(8,128)(2,1)S(1)} async-done(((bf16[16,2,8,3,256]{4,2,3,1,0:T(8,128)(2,1)}), bf16[16,2,8,3,256]{4,2,3,1,0:T(8,128)(2,1)S(1)}, u32[]{:S(2)}, u32[]{:S(2)}) %all-to-all-start) | async-done | bytes 393248 | tf_op jit(solution)/shard_map/all_to_all | solution.py:50
  32.4 1.1 copy.9
  33.5 177.9 %while.12 = (s32[]{:T(128)}, f32[4,1024,768]{2,1,0:T(8,128)}, s32[4,1024,256]{2,1,0:T(8,128)}, bf16[8,96,512]{2,1,0:T(8,128)(2,1)}, s32[]{:T(128)}) while((s32[]{:T(128)}, f32[4,1024,768]{2,1,0:T(8,128)}, s32[4,1024,256]{2,1,0:T(8,128)}, bf16[8,96,512]{2,1,0:T(8,128)(2,1)}, s32[]{:T(128)}) %tuple.37), condition=%wide.region_1.0_spmd, body=%wide.region_0.0_spmd.sunk | while | flops 855638016 | bytes 36438156 | solution.py:39
  33.5 1.3 dynamic-slice_bitcast_fusion.2
  34.8 33.8 %cosine_convert_fusion.2 = (bf16[8,1024,256]{2,1,0:T(8,128)(2,1)S(1)}, bf16[8,1024,256]{2,1,0:T(8,128)(2,1)S(1)}) fusion(s32[1024,256]{1,0:T(8,128)S(1)} %dynamic-slice_bitcast_fusion.2, s32[8]{0:T(128)S(1)} %multiply_add_fusion.2), kind=kLoop, calls=%fused_computation.13.clone.1 | loop fusion | flops 33554432 | bytes 9437216 | tf_op jit(solution)/shard_map/convert
  68.6 5.1 %fusion.15 = f32[8,1024,96]{1,2,0:T(8,128)} fusion(bf16[8,96,512]{2,1,0:T(8,128)(2,1)} %get-tuple-element.122, bf16[8,1024,256]{2,1,0:T(8,128)(2,1)S(1)} %get-tuple-element.107, bf16[8,1024,256]{2,1,0:T(8,128)(2,1)S(1)} %get-tuple-element.108), kind=kOutput, calls=%fused_computation.8.clone.1 | convolution fusion | flops 822083584 | bytes 12320768 | tf_op jit(solution)/shard_map/while/body/eval_jaxpr/frk,fwk->rfw/dot_general | solution.py:34
  73.7 2.4 copy.21
  76.1 1.9 constant_dynamic-update-slice_fusion.2
  78.0 1.3 dynamic-slice_bitcast_fusion.2
  79.3 33.8 %cosine_convert_fusion.2 = (bf16[8,1024,256]{2,1,0:T(8,128)(2,1)S(1)}, bf16[8,1024,256]{2,1,0:T(8,128)(2,1)S(1)}) fusion(s32[1024,256]{1,0:T(8,128)S(1)} %dynamic-slice_bitcast_fusion.2, s32[8]{0:T(128)S(1)} %multiply_add_fusion.2), kind=kLoop, calls=%fused_computation.13.clone.1 | loop fusion | flops 33554432 | bytes 9437216 | tf_op jit(solution)/shard_map/convert
  113.1 5.1 %fusion.15 = f32[8,1024,96]{1,2,0:T(8,128)} fusion(bf16[8,96,512]{2,1,0:T(8,128)(2,1)} %get-tuple-element.122, bf16[8,1024,256]{2,1,0:T(8,128)(2,1)S(1)} %get-tuple-element.107, bf16[8,1024,256]{2,1,0:T(8,128)(2,1)S(1)} %get-tuple-element.108), kind=kOutput, calls=%fused_computation.8.clone.1 | convolution fusion | flops 822083584 | bytes 12320768 | tf_op jit(solution)/shard_map/while/body/eval_jaxpr/frk,fwk->rfw/dot_general | solution.py:34
  118.2 2.4 copy.21
  120.6 1.9 constant_dynamic-update-slice_fusion.2
  122.5 1.3 dynamic-slice_bitcast_fusion.2
  123.8 33.8 %cosine_convert_fusion.2 = (bf16[8,1024,256]{2,1,0:T(8,128)(2,1)S(1)}, bf16[8,1024,256]{2,1,0:T(8,128)(2,1)S(1)}) fusion(s32[1024,256]{1,0:T(8,128)S(1)} %dynamic-slice_bitcast_fusion.2, s32[8]{0:T(128)S(1)} %multiply_add_fusion.2), kind=kLoop, calls=%fused_computation.13.clone.1 | loop fusion | flops 33554432 | bytes 9437216 | tf_op jit(solution)/shard_map/convert
  157.6 5.1 %fusion.15 = f32[8,1024,96]{1,2,0:T(8,128)} fusion(bf16[8,96,512]{2,1,0:T(8,128)(2,1)} %get-tuple-element.122, bf16[8,1024,256]{2,1,0:T(8,128)(2,1)S(1)} %get-tuple-element.107, bf16[8,1024,256]{2,1,0:T(8,128)(2,1)S(1)} %get-tuple-element.108), kind=kOutput, calls=%fused_computation.8.clone.1 | convolution fusion | flops 822083584 | bytes 12320768 | tf_op jit(solution)/shard_map/while/body/eval_jaxpr/frk,fwk->rfw/dot_general | solution.py:34
  162.7 2.4 copy.21
  165.1 1.9 constant_dynamic-update-slice_fusion.2
  167.0 1.3 dynamic-slice_bitcast_fusion.2
  168.3 33.8 %cosine_convert_fusion.2 = (bf16[8,1024,256]{2,1,0:T(8,128)(2,1)S(1)}, bf16[8,1024,256]{2,1,0:T(8,128)(2,1)S(1)}) fusion(s32[1024,256]{1,0:T(8,128)S(1)} %dynamic-slice_bitcast_fusion.2, s32[8]{0:T(128)S(1)} %multiply_add_fusion.2), kind=kLoop, calls=%fused_computation.13.clone.1 | loop fusion | flops 33554432 | bytes 9437216 | tf_op jit(solution)/shard_map/convert
  202.1 5.1 %fusion.15 = f32[8,1024,96]{1,2,0:T(8,128)} fusion(bf16[8,96,512]{2,1,0:T(8,128)(2,1)} %get-tuple-element.122, bf16[8,1024,256]{2,1,0:T(8,128)(2,1)S(1)} %get-tuple-element.107, bf16[8,1024,256]{2,1,0:T(8,128)(2,1)S(1)} %get-tuple-element.108), kind=kOutput, calls=%fused_computation.8.clone.1 | convolution fusion | flops 822083584 | bytes 12320768 | tf_op jit(solution)/shard_map/while/body/eval_jaxpr/frk,fwk->rfw/dot_general | solution.py:34
  207.2 2.4 copy.21
  209.6 1.8 constant_dynamic-update-slice_fusion.2
  211.7 34.7 %psum.7 = f32[48]{0:T(128)S(1)} all-reduce(f32[48]{0:T(128)S(1)} %reduce_sum.22), channel_id=1, replica_groups=mesh['grid'=16,'chan'=16] {'chan'}, use_global_device_ids=true, to_apply=%region_5.6 | all-reduce | flops 48 | bytes 384 | tf_op jit(solution)/shard_map/psum | solution.py:53
  246.4 92.9 %reduce-scatter.2.cloned.1.call-done = f32[256,768]{1,0:T(8,128)} async-done(((f32[4096,768]{1,0:T(8,128)}), f32[256,768]{1,0:T(8,128)}) %reduce-scatter.2.cloned.1.call-update) | async-done | bytes 786448 | tf_op jit(solution)/shard_map/reduce_scatter | solution.py:57
  339.3 1.5 integer_pow.10
  340.7 0.3 copy.11
  341.1 0.7 divide_bitcast_fusion
  (15 shorter events, 0.6 us)
Async XLA Ops:
  8.8 23.4 %all-to-all-start = ((bf16[16,2,8,3,256]{4,2,3,1,0:T(8,128)(2,1)}), bf16[16,2,8,3,256]{4,2,3,1,0:T(8,128)(2,1)S(1)}, u32[]{:S(2)}, u32[]{:S(2)}) async-start(bf16[16,2,8,3,256]{4,2,3,1,0:T(8,128)(2,1)} %stack.2), calls=%async_computation | async-start | bytes 786432 | tf_op jit(solution)/shard_map/all_to_all | solution.py:50
  18.9 320.4 %reduce-scatter.2.cloned.1.call-start = ((), (), s32[]{:S(2)}) async-start(), calls=%async_computation.2 | async-start | bytes 13369344 | tf_op jit(solution)/shard_map/reduce_scatter | solution.py:57
Sparse Core Ops, SparseCore 0:
  211.6 127.6 reduce-scatter.1
